TPU v7x, 256 devices: a whole 4x4x8 slice. The times are simulated.
256 devices in a mesh: ia: 4 (over y), ja: 4 (over x), ka: 16 (over z, core).
Axes of the slice: x: 4, y: 4, z: 8, core: 2. Of those that a mesh axis runs over, the one named last changes fastest.
Arguments:
- blocks: bfloat16 [4, 4, 16, 2, 128, 128, 128], P('ia', 'ja', 'ka'), may hold values from -6 to 6
- first_mode_rows: int32 [4, 4, 16, 2], P('ia', 'ja', 'ka'), may hold values from 0 to 15
- second_mode_rows: int32 [4, 4, 16, 2], P('ia', 'ja', 'ka'), may hold values from 0 to 15
- third_mode_rows: int32 [4, 4, 16, 2], P('ia', 'ja', 'ka'), may hold values from 0 to 3
- filled: int32 [4, 4, 16], P('ia', 'ja', 'ka'), may hold values from 1 to 2, as said below
- owner_one: int32 [64], replicated, may hold values from 0 to 63, each once
- owner_two: int32 [64], replicated, may hold values from 0 to 63, each once
- factor_b: float32 [4, 2048, 256], P('ja', ('ia', 'ka'))
- factor_c: float32 [16, 512, 256], P('ka')
Outputs:
- a_new: float32 [4, 2048, 256], P('ia', ('ja', 'ka'))
- b_new: float32 [4, 2048, 256], P('ja', ('ia', 'ka'))
Inputs may be any that keep to these rules, and one draw needn't show every extreme that they name: Number of nonempty slots of a grid cell; at least one cell has all 2 slots filled. Slots at or beyond this count hold data that is not part of the tensor.
All inputs are finite; a program needn't handle non-finite values.
Results may differ from a plain program's by a relative error of at most 0.0039.
The roundings to bfloat16 on the way count: a program that leaves them out, or rounds other values in their place, can miss the bound.
Values may be sent and summed in bfloat16 or wider, within the bound.
A program may use at most 128 MiB of HBM per device.

v0:
```python
import jax
import jax.numpy as jnp
from jax import lax
from jax.sharding import PartitionSpec as P

EPS = 1e-06


def solve_rows(gram, rows):
    lower = jnp.linalg.cholesky(gram)
    return jax.scipy.linalg.cho_solve((lower, True), rows.T).T


def add_rows(accum, start, contrib):
    current = lax.dynamic_slice_in_dim(accum, start, contrib.shape[0], 0)
    return lax.dynamic_update_slice_in_dim(accum, current + contrib, start, 0)


def batched_sum(inner, weights):
    summed = lax.dot_general(
        inner,
        weights.astype(jnp.float32),
        (((1,), (0,)), ((2,), (1,))),
        precision=lax.Precision.HIGHEST,
        preferred_element_type=jnp.float32,
    )
    return summed.T


def to_logical(stored, owner, piece_rows):
    return stored.reshape(-1, piece_rows, stored.shape[1])[owner].reshape(stored.shape)


def to_stored(logical, owner, piece_rows):
    positions = jnp.arange(owner.shape[0], dtype=jnp.int32)
    inverse = jnp.sum(
        jnp.where(owner[None, :] == positions[:, None], positions[None, :], 0), axis=1
    )
    return logical.reshape(-1, piece_rows, logical.shape[1])[inverse].reshape(logical.shape)


def keep_same(value):
    return value


def partial_value(function, slot):

    def applied(value):
        return function(value, slot)

    return applied


def body(
    blocks,
    first_mode_rows,
    second_mode_rows,
    third_mode_rows,
    filled,
    owner_one,
    owner_two,
    factor_b,
    factor_c,
):
    highest = lax.Precision.HIGHEST
    piece_rows = factor_b.shape[1]
    rank_width = factor_b.shape[2]
    block_edge = blocks.shape[-1]
    slot_count = blocks.shape[3]
    total_one = piece_rows * lax.axis_size("ia") * lax.axis_size("ja") * lax.axis_size("ka")
    slab_rows_one = piece_rows * lax.axis_size("ja") * lax.axis_size("ka")
    slab_rows_two = piece_rows * lax.axis_size("ia") * lax.axis_size("ka")
    own_b = factor_b[0]
    own_c = lax.dynamic_slice_in_dim(
        factor_c[0], lax.axis_index(("ia", "ja")) * piece_rows, piece_rows, 0
    )
    local_b = jnp.dot(own_b.T, own_b, precision=highest, preferred_element_type=jnp.float32)
    local_c = jnp.dot(own_c.T, own_c, precision=highest, preferred_element_type=jnp.float32)
    gram_b, gram_c = lax.psum((local_b, local_c), ("ia", "ja", "ka"))
    stored_b = lax.all_gather(factor_b.astype(jnp.bfloat16), ("ia", "ka"), axis=1, tiled=True)[0]
    half_b = to_logical(stored_b, owner_two, piece_rows)
    half_c = factor_c[0].astype(jnp.bfloat16)
    live_count = filled[0, 0, 0]

    def update_one(partial_sum, slot):
        block = blocks[0, 0, 0, slot]
        b_rows = lax.dynamic_slice_in_dim(
            half_b, second_mode_rows[0, 0, 0, slot] * block_edge, block_edge, 0
        )
        c_rows = lax.dynamic_slice_in_dim(
            half_c, third_mode_rows[0, 0, 0, slot] * block_edge, block_edge, 0
        )
        inner = jnp.dot(
            block.reshape(block_edge * block_edge, block_edge),
            c_rows,
            preferred_element_type=jnp.float32,
        )
        inner = inner.reshape(block_edge, block_edge, rank_width)
        contrib = batched_sum(inner, b_rows)
        return add_rows(partial_sum, first_mode_rows[0, 0, 0, slot] * block_edge, contrib)

    partial_one = jnp.zeros((slab_rows_one, rank_width), jnp.float32)
    for slot in range(slot_count):
        partial_one = lax.cond(
            slot < live_count, partial_value(update_one, slot), keep_same, partial_one
        )
    stored_one = to_stored(partial_one, owner_one, piece_rows)
    system_one = gram_b * gram_c
    summed_own = lax.psum_scatter(stored_one, ("ja", "ka"), scatter_dimension=0, tiled=True)
    a_hat = solve_rows(system_one, summed_own)
    squares_a = lax.psum(jnp.sum(a_hat * a_hat, axis=0), ("ia", "ja", "ka"))
    scale_a = jnp.sqrt(squares_a / total_one + EPS)
    a_own = a_hat / scale_a
    local_a = jnp.dot(a_own.T, a_own, precision=highest, preferred_element_type=jnp.float32)
    gram_a = lax.psum(local_a, ("ia", "ja", "ka"))
    stored_a = lax.all_gather(a_own.astype(jnp.bfloat16)[None], ("ja", "ka"), axis=1, tiled=True)[0]
    half_a = to_logical(stored_a, owner_one, piece_rows)

    def update_two(partial_sum, slot):
        block = blocks[0, 0, 0, slot]
        a_rows = lax.dynamic_slice_in_dim(
            half_a, first_mode_rows[0, 0, 0, slot] * block_edge, block_edge, 0
        )
        c_rows = lax.dynamic_slice_in_dim(
            half_c, third_mode_rows[0, 0, 0, slot] * block_edge, block_edge, 0
        )
        inner = lax.dot_general(
            block.reshape(block_edge, block_edge * block_edge),
            a_rows,
            (((0,), (0,)), ((), ())),
            preferred_element_type=jnp.float32,
        )
        inner = inner.reshape(block_edge, block_edge, rank_width)
        contrib = batched_sum(inner, c_rows)
        return add_rows(partial_sum, second_mode_rows[0, 0, 0, slot] * block_edge, contrib)

    partial_two = jnp.zeros((slab_rows_two, rank_width), jnp.float32)
    for slot in range(slot_count):
        partial_two = lax.cond(
            slot < live_count, partial_value(update_two, slot), keep_same, partial_two
        )
    stored_two = to_stored(partial_two, owner_two, piece_rows)
    summed_two = lax.psum_scatter(stored_two, ("ia", "ka"), scatter_dimension=0, tiled=True)
    b_hat = solve_rows(gram_a * gram_c, summed_two)
    squares_b = lax.psum(jnp.sum(b_hat * b_hat, axis=0), ("ia", "ja", "ka"))
    b_own = b_hat / jnp.sqrt(squares_b / total_one + EPS)
    return (a_own[None], b_own[None])


def solution(mesh):
    return jax.shard_map(
        body,
        mesh=mesh,
        in_specs=(
            P("ia", "ja", "ka", None, None, None, None),
            P("ia", "ja", "ka", None),
            P("ia", "ja", "ka", None),
            P("ia", "ja", "ka", None),
            P("ia", "ja", "ka"),
            P(),
            P(),
            P("ja", ("ia", "ka"), None),
            P("ka", None, None),
        ),
        out_specs=(P("ia", ("ja", "ka"), None), P("ja", ("ia", "ka"), None)),
        check_vma=False,
    )
```

profile of v0, /device:TPU:1, one launch (start us, length us, event | category | flops | bytes accessed | tf_op | source)
XLA Modules:
  0.0 827.5 jit_solution(4852424667202017735)
XLA Ops:
  17.5 75.5 %all-gather.4.cloned.1.call-done = bf16[1,2048,256]{2,1,0:T(8,128)(2,1)} async-done(((bf16[1,32,256]{2,1,0:T(8,128)(2,1)}), bf16[1,2048,256]{2,1,0:T(8,128)(2,1)}) %all-gather.4.cloned.1.call-update) | async-done | bytes 1048592 | tf_op jit(solution)/shard_map/all_gather | solution.py:80
  94.8 23.3 %conditional.4 = (f32[2048,256]{1,0:T(8,128)}) conditional(s32[]{:T(128)} %bitcast.41, () %tuple.54, (s32[1,1,1,2]{3,2,1,0:T(1,128)}, bf16[512,256]{1,0:T(8,128)(2,1)S(1)}, bf16[1,1,1,2,128,128,128]{6,5,4,3,2,1,0:T(8,128)(2,1)}, s32[1,1,1,2]{3,2,1,0:T(1,128)}, bf16[2048,256]{1,0:T(8,128)(2,1)S(1)}, /*index=5*/s32[1,1,1,2]{3,2,1,0:T(1,128)}) %tuple.134), branch_computations={%region_6.0_spmd, %region_7.0_spmd} | conditional | flops 1082130432 | bytes 83099928 | solution.py:104
  100.7 6.7 copy.52
  107.6 8.2 multiply_reduce_fusion
  118.1 3.6 gather_fusion.1
  122.1 149.6 %all-reduce.7.cloned.1.call-done = (f32[256,256]{0,1:T(8,128)}, f32[256,256]{0,1:T(8,128)}) async-done(((f32[256,256]{0,1:T(8,128)}, f32[256,256]{0,1:T(8,128)}), (f32[256,256]{0,1:T(8,128)}, f32[256,256]{0,1:T(8,128)})) %all-reduce.7.cloned.1.call-update) | async-done | bytes 524304 | tf_op jit(solution)/shard_map/psum | solution.py:79
  272.9 11.7 %cholesky.130 = f32[128,128]{1,0:T(8,128)S(1)} custom-call(f32[128,128]{1,0:T(8,128)S(1)} %cholesky.194), custom_call_target="Cholesky" | custom-call | tf_op jit(solution)/shard_map/jit(cholesky)/cholesky | solution.py:10
  284.7 9.8 %custom-call.15 = f32[1,128,128]{1,2,0:T(8,128)S(1)} custom-call(f32[1,128,128]{2,1,0:T(8,128)S(1)} %get-tuple-element.155), custom_call_target="InvertDiagBlocksLowerTriangular" | custom-call | tf_op jit(solution)/shard_map/jit(cholesky)/cholesky | solution.py:10
  295.0 11.7 %cholesky.147 = f32[128,128]{1,0:T(8,128)S(1)} custom-call(f32[128,128]{1,0:T(8,128)S(1)} %convolution_subtract_fusion.1), custom_call_target="Cholesky" | custom-call | tf_op jit(solution)/shard_map/jit(cholesky)/cholesky | solution.py:10
  308.8 14.6 %while.4 = (s32[]{:T(128)}, f32[256,256]{1,0:T(8,128)S(1)}, s32[2,2]{1,0:T(2,128)S(1)}, f32[2,128,128]{2,1,0:T(8,128)S(1)}, s32[]{:T(128)}) while((s32[]{:T(128)}, f32[256,256]{1,0:T(8,128)S(1)}, s32[2,2]{1,0:T(2,128)S(1)}, f32[2,128,128]{2,1,0:T(8,128)S(1)}, s32[]{:T(128)}) %tuple.103), condition=%wide.while_cond, body=%wide.while_body.sunk | while | flops 2 | bytes 131181 | solution.py:11
  323.4 19.7 %custom-call.16 = f32[2,128,128]{1,2,0:T(8,128)S(1)} custom-call(f32[2,128,128]{2,1,0:T(8,128)S(1)} %get-tuple-element.124), custom_call_target="InvertDiagBlocksLowerTriangular" | custom-call | tf_op jit(solution)/shard_map/jit(_cho_solve)/triangular_solve | solution.py:11
  345.9 77.9 %psum.37 = f32[256]{0:T(256)S(1)} all-reduce(f32[256]{0:T(256)S(1)} %multiply_reduce_fusion.5), channel_id=1, replica_groups=mesh['ia'=4,'ja'=4,'ka'=16] {'ia','ja','ka'}, use_global_device_ids=true, to_apply=%region_13.16 | all-reduce | flops 256 | bytes 2048 | tf_op jit(solution)/shard_map/psum | solution.py:111
  425.8 71.7 %all-gather.6.cloned.1.call-done = bf16[2048,256]{1,0:T(8,128)(2,1)} async-done(((bf16[32,256]{1,0:T(8,128)(2,1)}), bf16[2048,256]{1,0:T(8,128)(2,1)}) %all-gather.6.cloned.1.call-update) | async-done | bytes 1048592 | tf_op jit(solution)/shard_map/all_gather | solution.py:116
  499.4 23.6 %conditional.6 = (f32[2048,256]{1,0:T(8,128)}) conditional(s32[]{:T(128)} %bitcast.41, () %tuple.57, (s32[1,1,1,2]{3,2,1,0:T(1,128)S(1)}, bf16[2048,256]{1,0:T(8,128)(2,1)S(1)}, bf16[1,1,1,2,128,128,128]{6,5,4,3,2,1,0:T(8,128)(2,1)}, s32[1,1,1,2]{3,2,1,0:T(1,128)S(1)}, bf16[512,256]{1,0:T(8,128)(2,1)S(1)}, ...), branch_computations={%region_15.18_spmd, %region_16.19_spmd} | conditional | flops 1082130432 | bytes 83099800 | solution.py:139
  505.5 6.7 copy.55
  512.4 8.3 multiply_reduce_fusion.2
  523.1 3.7 gather_fusion.3
  526.8 150.8 %all-reduce.5.cloned.1.call-done = f32[256,256]{0,1:T(8,128)} async-done(((f32[256,256]{0,1:T(8,128)}), f32[256,256]{0,1:T(8,128)}) %all-reduce.5.cloned.1.call-update) | async-done | bytes 262160 | tf_op jit(solution)/shard_map/psum | solution.py:115
  678.8 11.7 %cholesky.164 = f32[128,128]{1,0:T(8,128)S(1)} custom-call(f32[128,128]{1,0:T(8,128)S(1)} %cholesky.197), custom_call_target="Cholesky" | custom-call | tf_op jit(solution)/shard_map/jit(cholesky)/cholesky | solution.py:10
  690.6 9.8 %custom-call.17 = f32[1,128,128]{1,2,0:T(8,128)S(1)} custom-call(f32[1,128,128]{2,1,0:T(8,128)S(1)} %get-tuple-element.151), custom_call_target="InvertDiagBlocksLowerTriangular" | custom-call | tf_op jit(solution)/shard_map/jit(cholesky)/cholesky | solution.py:10
  700.9 11.7 %cholesky.181 = f32[128,128]{1,0:T(8,128)S(1)} custom-call(f32[128,128]{1,0:T(8,128)S(1)} %convolution_subtract_fusion), custom_call_target="Cholesky" | custom-call | tf_op jit(solution)/shard_map/jit(cholesky)/cholesky | solution.py:10
  715.2 4.2 while.5
  719.4 19.7 %custom-call.18 = f32[2,128,128]{1,2,0:T(8,128)S(1)} custom-call(f32[2,128,128]{2,1,0:T(8,128)S(1)} %get-tuple-element.125), custom_call_target="InvertDiagBlocksLowerTriangular" | custom-call | tf_op jit(solution)/shard_map/jit(_cho_solve)/triangular_solve | solution.py:11
  742.0 77.3 %psum.39 = f32[256]{0:T(256)S(1)} all-reduce(f32[256]{0:T(256)S(1)} %multiply_reduce_fusion.4), channel_id=1, replica_groups=mesh['ia'=4,'ja'=4,'ka'=16] {'ia','ja','ka'}, use_global_device_ids=true, to_apply=%region_22.25 | all-reduce | flops 256 | bytes 2048 | tf_op jit(solution)/shard_map/psum | solution.py:145
  (117 shorter events, 50.5 us)
Async XLA Ops:
  8.0 85.0 %all-gather.4.cloned.1.call-start = ((), (), s32[]{:S(2)}) async-start(), calls=%async_computation.2 | async-start | bytes 1064960 | tf_op jit(solution)/shard_map/all_gather | solution.py:80
  9.4 262.2 %all-reduce.7.cloned.1.call-start = ((), (), s32[]{:S(2)}) async-start(), calls=%async_computation.7 | async-start | bytes 1048576 | tf_op jit(solution)/shard_map/psum | solution.py:79
  13.5 329.6 %reduce-scatter.3.cloned.1.call-start = ((), (), s32[]{:S(2)}) async-start(), calls=%async_computation.3 | async-start | bytes 2129920 | tf_op jit(solution)/shard_map/reduce_scatter | solution.py:109
  100.7 6.7 copy-start.4
  107.5 8.4 %copy-start.7 = (s32[1,1,1,2]{3,2,1,0:T(1,128)S(1)}, s32[1,1,1,2]{3,2,1,0:T(1,128)}, u32[]{:S(2)}) copy-start(s32[1,1,1,2]{3,2,1,0:T(1,128)} %get-tuple-element.85) | copy-start | bytes 28 | tf_op jit(solution)/shard_map/cond
  121.7 302.8 %copy-start.1 = (s32[64]{0:T(128)S(1)}, s32[64]{0:T(128)}, u32[]{:S(2)}) copy-start(s32[64]{0:T(128)} %param.25) | copy-start | bytes 772
  121.8 375.7 %all-gather.6.cloned.1.call-start = ((), (), s32[]{:S(2)}) async-start(), calls=%async_computation.6 | async-start | bytes 1064960 | tf_op jit(solution)/shard_map/all_gather | solution.py:116
  271.6 227.7 %copy-start.2 = (s32[1,1,1,2]{3,2,1,0:T(1,128)S(1)}, s32[1,1,1,2]{3,2,1,0:T(1,128)}, u32[]{:S(2)}) copy-start(s32[1,1,1,2]{3,2,1,0:T(1,128)} %param.23) | copy-start | bytes 28
  271.6 227.7 %copy-start.3 = (s32[1,1,1,2]{3,2,1,0:T(1,128)S(1)}, s32[1,1,1,2]{3,2,1,0:T(1,128)}, u32[]{:S(2)}) copy-start(s32[1,1,1,2]{3,2,1,0:T(1,128)} %param.22) | copy-start | bytes 28
  271.6 227.7 %copy-start.6 = (s32[1,1,1,2]{3,2,1,0:T(1,128)S(1)}, s32[1,1,1,2]{3,2,1,0:T(1,128)}, u32[]{:S(2)}) copy-start(s32[1,1,1,2]{3,2,1,0:T(1,128)} %param.21) | copy-start | bytes 28
  424.5 253.1 %all-reduce.5.cloned.1.call-start = ((), (), s32[]{:S(2)}) async-start(), calls=%async_computation.4 | async-start | bytes 524288 | tf_op jit(solution)/shard_map/psum | solution.py:115
  425.8 313.4 %reduce-scatter.5.cloned.1.call-start = ((), (), s32[]{:S(2)}) async-start(), calls=%async_computation.5 | async-start | bytes 2129920 | tf_op jit(solution)/shard_map/reduce_scatter | solution.py:143
  523.1 154.5 %copy-start = (f32[256,256]{0,1:T(8,128)S(1)}, f32[256,256]{0,1:T(8,128)}, u32[]{:S(2)}) copy-start(f32[256,256]{0,1:T(8,128)} %get-tuple-element.143) | copy-start | bytes 786436
Sparse Core Ops, SparseCore 0:
  12.2 80.7 all-gather.3
  121.9 159.1 reduce-scatter.2
  424.6 72.8 all-gather.5
  527.0 159.5 reduce-scatter.4
Sparse Core Ops, SparseCore 1:
  15.6 256.0 all-reduce.6
  431.3 246.2 all-reduce.4
where the time goes:
time: 837 us; the launch traced here: 827 us
  waiting for transfers between devices  448 us (54%)
  blocking collectives  155 us (19%)
  other arithmetic  133 us (16%)
  local copies, waits for them, and re-layouts  42.5 us (5%)
  between operations  19.3 us (2%)
  matrix products  17.4 us (2%)
  loops' own time  12.2 us (1%)
    psum x1, waiting for transfers between devices, body(): gram_a = lax.psum(local_a, ('ia', 'ja', 'ka'))  151 us
    psum x1, waiting for transfers between devices, body(): gram_b, gram_c = lax.psum((local_b, local_c), ('ia', 'ja', 'ka'))  150 us
    psum x1, blocking collectives, body(): squares_a = lax.psum(jnp.sum(a_hat * a_hat, axis=0), ('ia', 'ja', 'ka'))  77.9 us
    psum x1, blocking collectives, body(): squares_b = lax.psum(jnp.sum(b_hat * b_hat, axis=0), ('ia', 'ja', 'ka'))  77.3 us
    all_gather x1, waiting for transfers between devices, body(): lax.all_gather(factor_b.astype(jnp.bfloat16), ('ia', 'ka'), axis=1, tiled...  75.5 us
    all_gather x1, waiting for transfers between devices, body(): lax.all_gather(a_own.astype(jnp.bfloat16)[None], ('ja', 'ka'), axis=1, ti...  71.7 us
    another operation x13, other arithmetic, solve_rows(): lower = jnp.linalg.cholesky(gram)  68.6 us
    another operation x5, other arithmetic, solve_rows(): return jax.scipy.linalg.cho_solve((lower, True), rows.T).T  39.4 us
  transfers between devices with their start and end apart: 6, of which 4 were waited for; matrix products, arithmetic and copies ran while one was open for 22% of the time, Pallas kernels for 0%

commit v1 on v0

--- a/solution.py
+++ b/solution.py
@@ -77,7 +77,15 @@
     local_b = jnp.dot(own_b.T, own_b, precision=highest, preferred_element_type=jnp.float32)
     local_c = jnp.dot(own_c.T, own_c, precision=highest, preferred_element_type=jnp.float32)
     gram_b, gram_c = lax.psum((local_b, local_c), ("ia", "ja", "ka"))
-    stored_b = lax.all_gather(factor_b.astype(jnp.bfloat16), ("ia", "ka"), axis=1, tiled=True)[0]
+    stored_b = jnp.concatenate(
+        lax.all_to_all(
+            jnp.stack([factor_b.astype(jnp.bfloat16)] * lax.axis_size(("ia", "ka"))),
+            ("ia", "ka"),
+            0,
+            0,
+        ),
+        axis=1,
+    )[0]
     half_b = to_logical(stored_b, owner_two, piece_rows)
     half_c = factor_c[0].astype(jnp.bfloat16)
     live_count = filled[0, 0, 0]

time: 837 us -> 931 us (1.11)
  waiting for transfers between devices: 448 us -> 531 us
  starting transfers between devices: 0.51 us -> 13.4 us
    reduce_scatter x1, waiting for transfers between devices: 0.02 us -> 79.3 us  [body(): lax.psum_scatter(stored_two, ('ia', 'ka'), scatter_dimension=0, tiled=True)]
    all_gather x1 -> x0, waiting for transfers between devices: 75.5 us -> none  [body(): lax.all_gather(factor_b.astype(jnp.bfloat16), ('ia', 'ka'), axis=1, tiled...]
    psum x1, waiting for transfers between devices: 150 us -> 206 us  [body(): gram_b, gram_c = lax.psum((local_b, local_c), ('ia', 'ja', 'ka'))]
    all_to_all x0 -> x1, waiting for transfers between devices: none -> 23.7 us  [body(): lax.all_to_all(jnp.stack([factor_b.astype(jnp.bfloat16)] * lax.axis_size(...]
    all_to_all x0 -> x1, starting transfers between devices: none -> 13.2 us  [body(): lax.all_to_all(jnp.stack([factor_b.astype(jnp.bfloat16)] * lax.axis_size(...]
  transfers between devices with their start and end apart: 6 -> 6, of which waited for: 4 -> 5; matrix products, arithmetic and copies ran while one was open for 22% -> 20% of each run, Pallas kernels for 0% -> 0%
where the time goes in v1:
time: 931 us; the launch traced here: 922 us
  waiting for transfers between devices  531 us (57%)
  blocking collectives  157 us (17%)
  other arithmetic  129 us (14%)
  local copies, waits for them, and re-layouts  42.4 us (5%)
  between operations  19.4 us (2%)
  matrix products  17.4 us (2%)
  starting transfers between devices  13.4 us (1%)
  loops' own time  11.7 us (1%)
    psum x1, waiting for transfers between devices, body(): gram_b, gram_c = lax.psum((local_b, local_c), ('ia', 'ja', 'ka'))  206 us
    psum x1, waiting for transfers between devices, body(): gram_a = lax.psum(local_a, ('ia', 'ja', 'ka'))  151 us
    psum x1, blocking collectives, body(): squares_b = lax.psum(jnp.sum(b_hat * b_hat, axis=0), ('ia', 'ja', 'ka'))  79.5 us
    reduce_scatter x1, waiting for transfers between devices, body(): lax.psum_scatter(stored_two, ('ia', 'ka'), scatter_dimension=0, tiled=True)  79.3 us
    psum x1, blocking collectives, body(): squares_a = lax.psum(jnp.sum(a_hat * a_hat, axis=0), ('ia', 'ja', 'ka'))  77.6 us
    all_gather x1, waiting for transfers between devices, body(): lax.all_gather(a_own.astype(jnp.bfloat16)[None], ('ja', 'ka'), axis=1, ti...  71.8 us
    another operation x13, other arithmetic, solve_rows(): lower = jnp.linalg.cholesky(gram)  68.6 us
    another operation x5, other arithmetic, solve_rows(): return jax.scipy.linalg.cho_solve((lower, True), rows.T).T  39.4 us
  transfers between devices with their start and end apart: 6, of which 5 were waited for; matrix products, arithmetic and copies ran while one was open for 20% of the time, Pallas kernels for 0%

profile of v1, /device:TPU:1, one launch (start us, length us, event | category | flops | bytes accessed | tf_op | source)
XLA Modules:
  0.0 921.5 jit_solution(4666668900096133365)
XLA Ops:
  10.0 13.2 %all-to-all-start = ((bf16[64,1,32,256]{3,2,1,0:T(8,128)(2,1)}), bf16[64,1,32,256]{3,2,1,0:T(8,128)(2,1)S(1)}, u32[]{:S(2)}, u32[]{:S(2)}) async-start(bf16[64,1,32,256]{3,2,1,0:T(8,128)(2,1)} %stack.2), calls=%async_computation | async-start | bytes 2097152 | tf_op jit(solution)/shard_map/all_to_all | solution.py:81
  28.2 23.7 %all-to-all-done = bf16[64,1,32,256]{3,2,1,0:T(8,128)(2,1)S(1)} async-done(((bf16[64,1,32,256]{3,2,1,0:T(8,128)(2,1)}), bf16[64,1,32,256]{3,2,1,0:T(8,128)(2,1)S(1)}, u32[]{:S(2)}, u32[]{:S(2)}) %all-to-all-start) | async-done | bytes 1048608 | tf_op jit(solution)/shard_map/all_to_all | solution.py:81
  52.5 22.7 %conditional.4 = (f32[2048,256]{1,0:T(8,128)}) conditional(s32[]{:T(128)} %bitcast.41, () %tuple.54, (s32[1,1,1,2]{3,2,1,0:T(1,128)S(1)}, bf16[512,256]{1,0:T(8,128)(2,1)S(1)}, bf16[1,1,1,2,128,128,128]{6,5,4,3,2,1,0:T(8,128)(2,1)}, s32[1,1,1,2]{3,2,1,0:T(1,128)S(1)}, bf16[2048,256]{1,0:T(8,128)(2,1)S(1)}, ...), branch_computations={%region_6.0_spmd, %region_7.0_spmd} | conditional | flops 1082130432 | bytes 83099800 | solution.py:112
  57.8 6.7 copy.52
  64.7 8.3 multiply_reduce_fusion
  79.2 205.6 %all-reduce.7.cloned.1.call-done = (f32[256,256]{0,1:T(8,128)}, f32[256,256]{0,1:T(8,128)}) async-done(((f32[256,256]{0,1:T(8,128)}, f32[256,256]{0,1:T(8,128)}), (f32[256,256]{0,1:T(8,128)}, f32[256,256]{0,1:T(8,128)})) %all-reduce.7.cloned.1.call-update) | async-done | bytes 524304 | tf_op jit(solution)/shard_map/psum | solution.py:79
  286.0 11.7 %cholesky.130 = f32[128,128]{1,0:T(8,128)S(1)} custom-call(f32[128,128]{1,0:T(8,128)S(1)} %cholesky.194), custom_call_target="Cholesky" | custom-call | tf_op jit(solution)/shard_map/jit(cholesky)/cholesky | solution.py:10
  297.8 9.8 %custom-call.15 = f32[1,128,128]{1,2,0:T(8,128)S(1)} custom-call(f32[1,128,128]{2,1,0:T(8,128)S(1)} %get-tuple-element.155), custom_call_target="InvertDiagBlocksLowerTriangular" | custom-call | tf_op jit(solution)/shard_map/jit(cholesky)/cholesky | solution.py:10
  308.1 11.7 %cholesky.147 = f32[128,128]{1,0:T(8,128)S(1)} custom-call(f32[128,128]{1,0:T(8,128)S(1)} %convolution_subtract_fusion.1), custom_call_target="Cholesky" | custom-call | tf_op jit(solution)/shard_map/jit(cholesky)/cholesky | solution.py:10
  321.9 14.5 %while.4 = (s32[]{:T(128)}, f32[256,256]{1,0:T(8,128)S(1)}, s32[2,2]{1,0:T(2,128)S(1)}, f32[2,128,128]{2,1,0:T(8,128)S(1)}, s32[]{:T(128)}) while((s32[]{:T(128)}, f32[256,256]{1,0:T(8,128)S(1)}, s32[2,2]{1,0:T(2,128)S(1)}, f32[2,128,128]{2,1,0:T(8,128)S(1)}, s32[]{:T(128)}) %tuple.103), condition=%wide.while_cond, body=%wide.while_body.sunk | while | flops 2 | bytes 131181 | solution.py:11
  336.5 19.7 %custom-call.16 = f32[2,128,128]{1,2,0:T(8,128)S(1)} custom-call(f32[2,128,128]{2,1,0:T(8,128)S(1)} %get-tuple-element.124), custom_call_target="InvertDiagBlocksLowerTriangular" | custom-call | tf_op jit(solution)/shard_map/jit(_cho_solve)/triangular_solve | solution.py:11
  359.0 77.6 %psum.37 = f32[256]{0:T(256)S(1)} all-reduce(f32[256]{0:T(256)S(1)} %multiply_reduce_fusion.5), channel_id=1, replica_groups=mesh['ia'=4,'ja'=4,'ka'=16] {'ia','ja','ka'}, use_global_device_ids=true, to_apply=%region_13.16 | all-reduce | flops 256 | bytes 2048 | tf_op jit(solution)/shard_map/psum | solution.py:119
  438.6 71.8 %all-gather.3.cloned.1.call-done = bf16[2048,256]{1,0:T(8,128)(2,1)} async-done(((bf16[32,256]{1,0:T(8,128)(2,1)}), bf16[2048,256]{1,0:T(8,128)(2,1)}) %all-gather.3.cloned.1.call-update) | async-done | bytes 1048592 | tf_op jit(solution)/shard_map/all_gather | solution.py:124
  512.2 23.6 %conditional.6 = (f32[2048,256]{1,0:T(8,128)}) conditional(s32[]{:T(128)} %bitcast.41, () %tuple.57, (s32[1,1,1,2]{3,2,1,0:T(1,128)S(1)}, bf16[2048,256]{1,0:T(8,128)(2,1)S(1)}, bf16[1,1,1,2,128,128,128]{6,5,4,3,2,1,0:T(8,128)(2,1)}, s32[1,1,1,2]{3,2,1,0:T(1,128)S(1)}, bf16[512,256]{1,0:T(8,128)(2,1)S(1)}, ...), branch_computations={%region_15.18_spmd, %region_16.19_spmd} | conditional | flops 1082130432 | bytes 83099800 | solution.py:147
  518.4 6.7 copy.55
  525.2 8.3 multiply_reduce_fusion.2
  539.7 150.5 %all-reduce.5.cloned.1.call-done = f32[256,256]{0,1:T(8,128)} async-done(((f32[256,256]{0,1:T(8,128)}), f32[256,256]{0,1:T(8,128)}) %all-reduce.5.cloned.1.call-update) | async-done | bytes 262160 | tf_op jit(solution)/shard_map/psum | solution.py:123
  691.4 11.7 %cholesky.164 = f32[128,128]{1,0:T(8,128)S(1)} custom-call(f32[128,128]{1,0:T(8,128)S(1)} %cholesky.197), custom_call_target="Cholesky" | custom-call | tf_op jit(solution)/shard_map/jit(cholesky)/cholesky | solution.py:10
  703.2 9.8 %custom-call.17 = f32[1,128,128]{1,2,0:T(8,128)S(1)} custom-call(f32[1,128,128]{2,1,0:T(8,128)S(1)} %get-tuple-element.151), custom_call_target="InvertDiagBlocksLowerTriangular" | custom-call | tf_op jit(solution)/shard_map/jit(cholesky)/cholesky | solution.py:10
  713.5 11.7 %cholesky.181 = f32[128,128]{1,0:T(8,128)S(1)} custom-call(f32[128,128]{1,0:T(8,128)S(1)} %convolution_subtract_fusion), custom_call_target="Cholesky" | custom-call | tf_op jit(solution)/shard_map/jit(cholesky)/cholesky | solution.py:10
  727.8 4.2 while.5
  732.0 19.7 %custom-call.18 = f32[2,128,128]{1,2,0:T(8,128)S(1)} custom-call(f32[2,128,128]{2,1,0:T(8,128)S(1)} %get-tuple-element.125), custom_call_target="InvertDiagBlocksLowerTriangular" | custom-call | tf_op jit(solution)/shard_map/jit(_cho_solve)/triangular_solve | solution.py:11
  751.7 79.3 %reduce-scatter.5.cloned.1.call-done = f32[32,256]{1,0:T(8,128)} async-done(((f32[2048,256]{1,0:T(8,128)}), f32[32,256]{1,0:T(8,128)}) %reduce-scatter.5.cloned.1.call-update) | async-done | bytes 32784 | tf_op jit(solution)/shard_map/reduce_scatter | solution.py:151
  833.8 79.5 %psum.39 = f32[256]{0:T(256)S(1)} all-reduce(f32[256]{0:T(256)S(1)} %multiply_reduce_fusion.4), channel_id=1, replica_groups=mesh['ia'=4,'ja'=4,'ka'=16] {'ia','ja','ka'}, use_global_device_ids=true, to_apply=%region_22.25 | all-reduce | flops 256 | bytes 2048 | tf_op jit(solution)/shard_map/psum | solution.py:153
  (117 shorter events, 54.0 us)
Async XLA Ops:
  8.0 20.2 %copy-start.1 = (f32[1,512,256]{2,1,0:T(8,128)S(1)}, f32[1,512,256]{2,1,0:T(8,128)}, u32[]{:S(2)}) copy-start(f32[1,512,256]{2,1,0:T(8,128)} %param.28) | copy-start | bytes 1572868
  8.0 19.2 %copy-start.2 = (s32[64]{0:T(128)S(1)}, s32[64]{0:T(128)}, u32[]{:S(2)}) copy-start(s32[64]{0:T(128)} %param.26) | copy-start | bytes 772
  8.0 19.4 %copy-start.3 = (s32[64]{0:T(128)S(1)}, s32[64]{0:T(128)}, u32[]{:S(2)}) copy-start(s32[64]{0:T(128)} %param.25) | copy-start | bytes 772
  8.0 44.5 %copy-start.6 = (s32[1,1,1,2]{3,2,1,0:T(1,128)S(1)}, s32[1,1,1,2]{3,2,1,0:T(1,128)}, u32[]{:S(2)}) copy-start(s32[1,1,1,2]{3,2,1,0:T(1,128)} %param.21) | copy-start | bytes 28
  8.0 44.5 %copy-start.5 = (s32[1,1,1,2]{3,2,1,0:T(1,128)S(1)}, s32[1,1,1,2]{3,2,1,0:T(1,128)}, u32[]{:S(2)}) copy-start(s32[1,1,1,2]{3,2,1,0:T(1,128)} %param.22) | copy-start | bytes 28
  8.1 44.5 %copy-start.4 = (s32[1,1,1,2]{3,2,1,0:T(1,128)S(1)}, s32[1,1,1,2]{3,2,1,0:T(1,128)}, u32[]{:S(2)}) copy-start(s32[1,1,1,2]{3,2,1,0:T(1,128)} %param.23) | copy-start | bytes 28
  10.0 41.9 %all-to-all-start = ((bf16[64,1,32,256]{3,2,1,0:T(8,128)(2,1)}), bf16[64,1,32,256]{3,2,1,0:T(8,128)(2,1)S(1)}, u32[]{:S(2)}, u32[]{:S(2)}) async-start(bf16[64,1,32,256]{3,2,1,0:T(8,128)(2,1)} %stack.2), calls=%async_computation | async-start | bytes 2097152 | tf_op jit(solution)/shard_map/all_to_all | solution.py:81
  23.2 261.6 %all-reduce.7.cloned.1.call-start = ((), (), s32[]{:S(2)}) async-start(), calls=%async_computation.7 | async-start | bytes 1048576 | tf_op jit(solution)/shard_map/psum | solution.py:79
  27.2 329.0 %reduce-scatter.3.cloned.1.call-start = ((), (), s32[]{:S(2)}) async-start(), calls=%async_computation.3 | async-start | bytes 2129920 | tf_op jit(solution)/shard_map/reduce_scatter | solution.py:117
  79.1 431.3 %all-gather.3.cloned.1.call-start = ((), (), s32[]{:S(2)}) async-start(), calls=%async_computation.6 | async-start | bytes 1064960 | tf_op jit(solution)/shard_map/all_gather | solution.py:124
  437.3 253.0 %all-reduce.5.cloned.1.call-start = ((), (), s32[]{:S(2)}) async-start(), calls=%async_computation.4 | async-start | bytes 524288 | tf_op jit(solution)/shard_map/psum | solution.py:123
  438.5 392.5 %reduce-scatter.5.cloned.1.call-start = ((), (), s32[]{:S(2)}) async-start(), calls=%async_computation.5 | async-start | bytes 2129920 | tf_op jit(solution)/shard_map/reduce_scatter | solution.py:151
  536.0 154.2 %copy-start = (f32[256,256]{0,1:T(8,128)S(1)}, f32[256,256]{0,1:T(8,128)}, u32[]{:S(2)}) copy-start(f32[256,256]{0,1:T(8,128)} %get-tuple-element.143) | copy-start | bytes 786436
Sparse Core Ops, SparseCore 0:
  29.6 255.1 all-reduce.6
  444.5 245.7 all-reduce.4
  694.8 136.1 reduce-scatter.4
Sparse Core Ops, SparseCore 1:
  79.2 158.1 reduce-scatter.2
  437.3 73.0 all-gather.2
